TPU v7x, 256 devices: a whole 4x4x8 slice. The times are simulated.
256 devices in a mesh: row: 8 (over z), col: 32 (over x, y, core).
Axes of the slice: x: 4, y: 4, z: 8, core: 2. Of those that a mesh axis runs over, the one named last changes fastest.
Arguments:
- three_index: float32 [256, 512, 1024], P('col', None, 'row'), may hold values from -1.2 to 1.2
- occ_energy: float32 [256], replicated, may hold values from -2 to -0.5
- vir_energy: float32 [512], replicated, may hold values from 0.5 to 3
- block_mask: int32 [256, 8, 16], replicated, may hold values from 0 to 1, as said below
- pair_list: int32 [256, 4], P('col'), may hold values from -1 to 3, as said below
Outputs:
- response_density: float32 [256, 512, 1024], P('col', None, 'row')
- virtual_density: float32 [512, 512], replicated
Inputs may be any that keep to these rules, and one draw needn't show every extreme that they name: `block_mask`: each orbital keeps between 32 and 64 of its 128 blocks; some orbital keeps exactly 64. `pair_list`: in each row the live entries come first and are distinct, then -1; every orbital lists at least one partner class; some orbital lists 4.
All inputs are finite; a program needn't handle non-finite values.
Results may differ from a plain program's by a relative error of at most 0.0003.
Values sent between devices are 32-bit elements; how exact they have to be, the bound alone decides.
A program may use at most 128 MiB of HBM per device.

v0:
```python
import jax
import jax.numpy as jnp
from jax import lax
from jax.sharding import PartitionSpec as P

NVIR = 512
NAUX = 1024
BLOCK = 64
STEPS = 2
PAIRS_DEV = 4


def spread(block, axis, holder):
    block = jnp.where(lax.axis_index(axis) == holder, block, jnp.zeros_like(block))
    return lax.psum(block, axis)


def expand_mask(block_rows):
    widened = jnp.repeat(block_rows.astype(jnp.float32), BLOCK, axis=-2)
    return jnp.repeat(widened, BLOCK, axis=-1)


def pair_terms(own_rows, partner, energy_own, energy_partner, virtual):
    cross_term = lax.dot_general(
        own_rows,
        partner,
        (((1,), (1,)), ((), ())),
        precision=lax.Precision.HIGHEST,
        preferred_element_type=jnp.float32,
    )
    denominator = energy_own + energy_partner - virtual[:, None] - virtual[None, :]
    amplitude = cross_term / denominator
    weighted = 2.0 * amplitude - amplitude.T
    response = jnp.dot(
        weighted, partner, precision=lax.Precision.HIGHEST, preferred_element_type=jnp.float32
    )
    virt_density = lax.dot_general(
        weighted,
        amplitude,
        (((1,), (1,)), ((), ())),
        precision=lax.Precision.HIGHEST,
        preferred_element_type=jnp.float32,
    )
    return (response, virt_density)


def on_device(three_index, occ_energy, vir_energy, block_mask, pair_list):
    row_index = lax.axis_index("row")
    col_index = lax.axis_index("col")
    row_count = lax.axis_size("row")
    col_count = lax.axis_size("col")
    own_orbital = col_index * row_count + row_index
    gathered = lax.all_to_all(three_index, "row", split_axis=0, concat_axis=2, tiled=True)
    own_rows = gathered[0] * expand_mask(block_mask[own_orbital])
    panels = []
    for owner_step in range(STEPS):
        first_root = 2 * owner_step
        second_root = first_root + 1
        panels.append(spread(own_rows, "col", first_root))
        panels.append(spread(own_rows, "col", second_root))
    stacked = jnp.stack(panels)
    energy_own = occ_energy[own_orbital]
    response_sum = jnp.zeros((NVIR, NAUX), jnp.float32)
    density_sum = jnp.zeros((NVIR, NVIR), jnp.float32)
    for slot_index in range(PAIRS_DEV):
        listed = pair_list[row_index, slot_index]
        panel_index = jnp.maximum(listed, 0)
        partner = stacked[panel_index]
        energy_partner = occ_energy[panel_index * row_count + row_index]
        live = (listed >= 0).astype(jnp.float32)
        response, virt_density = pair_terms(
            own_rows, partner, energy_own, energy_partner, vir_energy
        )
        response = live * response
        virt_density = live * virt_density
        response_sum = response_sum + response
        density_sum = density_sum + virt_density
    returned = lax.all_to_all(response_sum[None], "row", split_axis=2, concat_axis=0, tiled=True)
    total = lax.psum(density_sum, ("row", "col"))
    return (returned, total / (row_count * col_count))


def solution(mesh):
    placed = (P("col", None, "row"), P(), P(), P(), P("col", None))
    return jax.shard_map(
        on_device,
        mesh=mesh,
        in_specs=placed,
        out_specs=(P("col", None, "row"), P()),
        check_vma=False,
    )
```

profile of v0, /device:TPU:2, one launch (start us, length us, event | category | flops | bytes accessed | tf_op | source)
XLA Modules:
  0.0 567.0 jit_solution(334607822717897980)
XLA Ops:
  7.2 0.0 copy-start
  7.2 2.9 copy.21
  10.1 8.5 %all-to-all-start = ((f32[8,512,128]{1,2,0:T(8,128)}), f32[8,512,128]{1,2,0:T(8,128)S(1)}, u32[]{:S(2)}, u32[]{:S(2)}) async-start(f32[8,512,128]{1,2,0:T(8,128)} %copy.21), calls=%async_computation | async-start | bytes 4194304 | tf_op jit(solution)/shard_map/all_to_all | solution.py:53
  18.6 0.0 all-reduce.6.cloned.1.call-start
  18.6 0.0 copy-done
  18.6 0.1 constant_dynamic-slice_fusion
  18.7 0.1 copy.30
  18.8 0.1 copy.23
  18.9 0.1 broadcast_in_dim.6
  19.0 0.1 reshape.59
  19.1 50.7 %all-to-all-done = f32[8,512,128]{1,2,0:T(8,128)S(1)} async-done(((f32[8,512,128]{1,2,0:T(8,128)}), f32[8,512,128]{1,2,0:T(8,128)S(1)}, u32[]{:S(2)}, u32[]{:S(2)}) %all-to-all-start) | async-done | bytes 2097184 | tf_op jit(solution)/shard_map/all_to_all | solution.py:53
  69.8 3.9 select_bitcast_fusion
  73.7 0.0 copy-done.1
  73.7 0.0 all-reduce.6.cloned.1.call-update
  73.8 0.6 copy-done.18
  74.4 0.7 constant_dynamic-slice_fusion.1
  80.1 0.0 copy-done.17
  80.2 0.7 fusion.49
  85.8 0.0 copy-done.19
  85.8 0.3 broadcast_in_dim.7
  86.0 2.2 bitcast_multiply_fusion.1
  88.2 111.9 %all-reduce.6.cloned.1.call-done = (f32[1,512,1024]{1,2,0:T(8,128)}, f32[1,512,1024]{1,2,0:T(8,128)}, f32[1,512,1024]{1,2,0:T(8,128)}, f32[1,512,1024]{1,2,0:T(8,128)}) async-done(((f32[1,512,1024]{1,2,0:T(8,128)}, f32[1,512,1024]{1,2,0:T(8,128)}, f32[1,512,1024]{1,2,0:T(8,128)}, f32[1,512,1024]{1,2,0:T(8,128)}), (f32[1,512,1024]{1,2,0:T(8,128)}, f32[1,512,1024]{1,2,0:T(8,128)}, f32[1,512,1024]{1,2,0:T(8,128)}, ...) | async-done | bytes 8388624 | tf_op jit(solution)/shard_map/psum | solution.py:15
  200.2 1.9 constant_dynamic-update-slice_fusion.3
  202.1 0.3 copy-done.10
  202.4 0.2 constant_dynamic-update-slice_fusion.2
  202.6 1.4 copy-done.9
  204.0 0.2 constant_dynamic-update-slice_fusion.1
  204.2 1.4 copy-done.8
  205.6 0.2 constant_dynamic-update-slice_fusion
  205.8 0.0 copy-start.2
  205.8 3.5 fusion.2
  209.3 4.6 fusion.6
  213.9 4.9 fusion.10
  218.7 0.0 copy-done.2
  218.7 4.5 fusion.14
  223.3 2.7 copy.24
  225.9 0.0 copy-done.5
  225.9 1.3 copy.25
  227.3 0.0 copy-done.3
  227.3 1.3 copy.26
  228.6 1.3 copy.27
  229.9 9.2 %fusion.8 = f32[512,1024]{1,0:T(8,128)S(1)} fusion(f32[4,512,1024]{1,2,0:T(8,128)} %copy-done.2, s32[]{:T(128)} %bitcast.18, f32[512,512]{1,0:T(8,128)S(1)} %copy-done.5, f32[512]{0:T(512)S(1)} %get-tuple-element.11, f32[512]{0:T(512)S(1)} %copy-done.19, f32[512,512]{0,1:T(8,128)} %copy.25), kind=kOutput, calls=%fused_computation.9 | convolution fusion | flops 3222798336 | bytes 6300160 | tf_op jit(solution)/shard_map/dot_general | solution.py:34
  239.1 0.0 copy-done.13
  239.1 0.0 slice-start.1
  239.1 0.0 copy-start.11
  239.1 8.7 %fusion.4 = f32[512,1024]{1,0:T(8,128)S(1)} fusion(f32[4,512,1024]{1,2,0:T(8,128)} %copy-done.2, s32[]{:T(128)} %bitcast.23, f32[512,512]{1,0:T(8,128)S(1)} %copy-done.3, f32[512]{0:T(512)S(1)} %get-tuple-element.13, f32[512]{0:T(512)S(1)} %copy-done.19, f32[512,512]{0,1:T(8,128)S(1)} %copy-done.13), kind=kOutput, calls=%fused_computation.5 | convolution fusion | flops 3222798336 | bytes 6300160 | tf_op jit(solution)/shard_map/dot_general | solution.py:34
  247.9 7.2 %fusion = f32[512,1024]{1,0:T(8,128)S(1)} fusion(f32[4,512,1024]{1,2,0:T(8,128)S(1)} %bitcast.112, s32[]{:T(128)} %bitcast.28, f32[512,512]{1,0:T(8,128)S(1)} %fusion.2, f32[512]{0:T(512)S(1)} %get-tuple-element.12, f32[512]{0:T(512)S(1)} %copy-done.19, f32[512,512]{0,1:T(8,128)S(1)} %copy-done.11), kind=kOutput, calls=%fused_computation.1 | convolution fusion | flops 3222798336 | bytes 6299652 | tf_op jit(solution)/shard_map/dot_general | solution.py:34
  255.1 7.2 %add_bitcast_fusion = f32[1,512,1024]{2,1,0:T(8,128)S(1)} fusion(f32[512,1024]{1,0:T(8,128)S(1)} %fusion, f32[512,1024]{1,0:T(8,128)S(1)} %fusion.4, f32[512,1024]{1,0:T(8,128)S(1)} %fusion.8, f32[4,512,1024]{1,2,0:T(8,128)S(1)} %bitcast.112, s32[]{:T(128)} %bitcast.13, f32[]{:T(128)} %bitcast.27, f32[]{:T(128)} %bitcast.22, f32[]{:T(128)} %bitcast.17, ...), kind=kOutput, calls=%fused_computation.18 | convolution fusion | flops 3226468352 | bytes 12591124 | tf_op jit(solution)/shard_map/dot_general | solution.py:34
  262.3 3.7 copy.28
  266.0 7.0 %all-to-all-start.1 = ((f32[1,512,1024]{1,0,2:T(1,128)}), f32[1,512,1024]{1,0,2:T(1,128)S(1)}, u32[]{:S(2)}, u32[]{:S(2)}) async-start(f32[1,512,1024]{1,0,2:T(1,128)} %copy.28), calls=%async_computation.1 | async-start | bytes 4194304 | tf_op jit(solution)/shard_map/all_to_all | solution.py:78
  273.0 0.3 all-reduce.4.cloned.1.call-start
  273.3 0.0 copy-start.6
  273.3 0.0 copy-start.15
  273.3 4.5 convolution_multiply_fusion.3
  277.8 2.5 fusion.28
  280.3 0.0 copy-start.12
  280.4 2.5 fusion.27
  282.9 0.0 copy-done.12
  282.9 3.5 fusion.26
  286.3 0.0 all-reduce.4.cloned.1.call-update
  286.4 267.5 %all-reduce.4.cloned.1.call-done = f32[512,512]{1,0:T(8,128)} async-done(((f32[512,512]{1,0:T(8,128)}), f32[512,512]{1,0:T(8,128)}) %all-reduce.4.cloned.1.call-update) | async-done | bytes 1048592 | tf_op jit(solution)/shard_map/psum | solution.py:79
  553.9 2.3 broadcast_multiply_fusion
  556.2 0.0 all-to-all-done.1
  556.2 3.6 copy.29
  (27 shorter events, 0.1 us)
Async XLA Ops:
  7.2 11.5 %copy-start = (s32[256,8,16]{0,2,1:T(8,128)S(1)}, s32[256,8,16]{0,2,1:T(8,128)}, u32[]{:S(2)}) copy-start(s32[256,8,16]{0,2,1:T(8,128)} %param.8) | copy-start | bytes 393220
  10.1 59.7 %all-to-all-start = ((f32[8,512,128]{1,2,0:T(8,128)}), f32[8,512,128]{1,2,0:T(8,128)S(1)}, u32[]{:S(2)}, u32[]{:S(2)}) async-start(f32[8,512,128]{1,2,0:T(8,128)} %copy.21), calls=%async_computation | async-start | bytes 4194304 | tf_op jit(solution)/shard_map/all_to_all | solution.py:53
  18.6 181.6 %all-reduce.6.cloned.1.call-start = ((), (), s32[]{:S(2)}) async-start(), calls=%async_computation.3 | async-start | bytes 16777216 | tf_op jit(solution)/shard_map/psum | solution.py:15
  69.8 4.0 copy-start.1
  73.7 0.7 copy-start.18
  73.7 6.4 %copy-start.17 = (f32[256]{0:T(256)S(1)}, f32[256]{0:T(256)}, u32[]{:S(2)}) copy-start(f32[256]{0:T(256)} %param.6) | copy-start | bytes 3076
  73.7 12.0 %copy-start.19 = (f32[512]{0:T(512)S(1)}, f32[512]{0:T(512)}, u32[]{:S(2)}) copy-start(f32[512]{0:T(512)} %param.7) | copy-start | bytes 6148
  200.2 2.2 copy-start.10
  202.4 1.6 copy-start.9
  204.0 1.6 copy-start.8
  205.8 13.0 %copy-start.2 = (f32[4,512,1024]{1,2,0:T(8,128)}, f32[4,512,1024]{1,2,0:T(8,128)S(1)}, u32[]{:S(2)}) copy-start(f32[4,512,1024]{1,2,0:T(8,128)S(1)} %constant_dynamic-update-slice_fusion) | copy-start | bytes 25165828
  223.2 2.7 copy-start.5
  223.2 4.0 copy-start.3
  229.9 9.2 %copy-start.13 = (f32[512,512]{0,1:T(8,128)S(1)}, f32[512,512]{0,1:T(8,128)}, u32[]{:S(2)}) copy-start(f32[512,512]{0,1:T(8,128)} %copy.26) | copy-start | bytes 3145732
  229.9 17.9 %slice-start = ((s8[8388608]{0:T(1024)(128)(4,1)}), s8[4194304]{0:T(1024)(128)(4,1)S(1)}, s32[]{:S(2)}) async-start(s8[8388608]{0:T(1024)(128)(4,1)} %bitcast.111), calls=%async_computation.4 | async-start | bytes 8388608
  239.1 8.7 %slice-start.1 = ((s8[8388608]{0:T(1024)(128)(4,1)}), s8[4194304]{0:T(1024)(128)(4,1)S(1)}, s32[]{:S(2)}) async-start(s8[8388608]{0:T(1024)(128)(4,1)} %bitcast.111), calls=%async_computation.5 | async-start | bytes 8388608
  239.1 8.7 %copy-start.11 = (f32[512,512]{0,1:T(8,128)S(1)}, f32[512,512]{0,1:T(8,128)}, u32[]{:S(2)}) copy-start(f32[512,512]{0,1:T(8,128)} %copy.27) | copy-start | bytes 3145732
  247.9 7.2 %copy-start.7 = (f32[512,512]{1,0:T(8,128)S(1)}, f32[512,512]{1,0:T(8,128)}, u32[]{:S(2)}) copy-start(f32[512,512]{1,0:T(8,128)} %fusion.14) | copy-start | bytes 3145732
  247.9 7.2 %copy-start.16 = (f32[512,512]{0,1:T(8,128)S(1)}, f32[512,512]{0,1:T(8,128)}, u32[]{:S(2)}) copy-start(f32[512,512]{0,1:T(8,128)} %copy.24) | copy-start | bytes 3145732
  266.0 290.2 %all-to-all-start.1 = ((f32[1,512,1024]{1,0,2:T(1,128)}), f32[1,512,1024]{1,0,2:T(1,128)S(1)}, u32[]{:S(2)}, u32[]{:S(2)}) async-start(f32[1,512,1024]{1,0,2:T(1,128)} %copy.28), calls=%async_computation.1 | async-start | bytes 4194304 | tf_op jit(solution)/shard_map/all_to_all | solution.py:78
  273.0 280.9 %all-reduce.4.cloned.1.call-start = ((), (), s32[]{:S(2)}) async-start(), calls=%async_computation.2 | async-start | bytes 2097152 | tf_op jit(solution)/shard_map/psum | solution.py:79
  273.3 4.5 copy-start.6
  273.3 4.5 copy-start.15
  277.8 2.5 copy-start.4
  277.8 2.5 copy-start.14
  280.3 2.5 copy-start.12
Sparse Core Ops, SparseCore 0:
  73.9 126.2 all-reduce.5
  286.5 267.3 all-reduce.3
where the time goes:
time: 576 us; the launch traced here: 567 us
  waiting for transfers between devices  430 us (75%)
  matrix products  62.6 us (11%)
  local copies, waits for them, and re-layouts  25.2 us (4%)
  between operations  24.9 us (4%)
  starting transfers between devices  15.8 us (3%)
  other arithmetic  8.42 us (1%)
    psum x1, waiting for transfers between devices, on_device(): total = lax.psum(density_sum, ('row', 'col'))  267 us
    psum x1, waiting for transfers between devices, spread(): return lax.psum(block, axis)  112 us
    all_to_all x1, waiting for transfers between devices, on_device(): lax.all_to_all(three_index, 'row', split_axis=0, concat_axis=2, tiled=True)  50.7 us
    dot_general x4, matrix products, pair_terms(): jnp.dot(weighted, partner, precision=lax.Precision.HIGHEST, preferred_ele...  32.2 us
    dot_general x4, matrix products, pair_terms(): lax.dot_general(own_rows, partner, (((1,), (1,)), ((), ())), precision=la...  17.5 us
    dot_general x4, matrix products, pair_terms(): lax.dot_general(weighted, amplitude, (((1,), (1,)), ((), ())), precision=...  12.9 us
  transfers between devices with their start and end apart: 4, of which 3 were waited for; matrix products, arithmetic and copies ran while one was open for 3% of the time, Pallas kernels for 0%

commit v1 on v0

--- a/solution.py
+++ b/solution.py
@@ -76,7 +76,7 @@
         response_sum = response_sum + response
         density_sum = density_sum + virt_density
     returned = lax.all_to_all(response_sum[None], "row", split_axis=2, concat_axis=0, tiled=True)
-    total = lax.psum(density_sum, ("row", "col"))
+    total = lax.psum(lax.psum(density_sum, "row"), "col")
     return (returned, total / (row_count * col_count))
 
 

time: 576 us -> 514 us (0.89)
  the two profiles are of different devices: /device:TPU:2 before, /device:TPU:1 now
where the time goes in v1:
time: 514 us; the launch traced here: 505 us
  waiting for transfers between devices  368 us (72%)
  matrix products  62.6 us (12%)
  local copies, waits for them, and re-layouts  25.2 us (5%)
  between operations  24.6 us (5%)
  starting transfers between devices  16.1 us (3%)
  other arithmetic  8.42 us (2%)
    psum x2, waiting for transfers between devices, on_device(): total = lax.psum(lax.psum(density_sum, 'row'), 'col')  204 us
    psum x1, waiting for transfers between devices, spread(): return lax.psum(block, axis)  112 us
    all_to_all x1, waiting for transfers between devices, on_device(): lax.all_to_all(three_index, 'row', split_axis=0, concat_axis=2, tiled=True)  51.1 us
    dot_general x4, matrix products, pair_terms(): jnp.dot(weighted, partner, precision=lax.Precision.HIGHEST, preferred_ele...  32.2 us
    dot_general x4, matrix products, pair_terms(): lax.dot_general(own_rows, partner, (((1,), (1,)), ((), ())), precision=la...  17.5 us
    dot_general x4, matrix products, pair_terms(): lax.dot_general(weighted, amplitude, (((1,), (1,)), ((), ())), precision=...  12.9 us
  transfers between devices with their start and end apart: 5, of which 4 were waited for; matrix products, arithmetic and copies ran while one was open for 4% of the time, Pallas kernels for 0%

profile of v1, /device:TPU:1, one launch (start us, length us, event | category | flops | bytes accessed | tf_op | source)
XLA Modules:
  0.0 504.5 jit_solution(13505209922436045203)
XLA Ops:
  7.2 0.0 copy-start
  7.2 2.9 copy.21
  10.1 9.0 %all-to-all-start = ((f32[8,512,128]{1,2,0:T(8,128)}), f32[8,512,128]{1,2,0:T(8,128)S(1)}, u32[]{:S(2)}, u32[]{:S(2)}) async-start(f32[8,512,128]{1,2,0:T(8,128)} %copy.21), calls=%async_computation | async-start | bytes 4194304 | tf_op jit(solution)/shard_map/all_to_all | solution.py:53
  19.1 0.0 all-reduce.9.cloned.1.call-start
  19.2 0.0 copy-done
  19.2 0.1 constant_dynamic-slice_fusion
  19.3 0.1 copy.30
  19.4 0.1 copy.23
  19.5 0.1 broadcast_in_dim.6
  19.5 0.1 reshape.59
  19.6 51.1 %all-to-all-done = f32[8,512,128]{1,2,0:T(8,128)S(1)} async-done(((f32[8,512,128]{1,2,0:T(8,128)}), f32[8,512,128]{1,2,0:T(8,128)S(1)}, u32[]{:S(2)}, u32[]{:S(2)}) %all-to-all-start) | async-done | bytes 2097184 | tf_op jit(solution)/shard_map/all_to_all | solution.py:53
  70.8 3.9 select_bitcast_fusion
  74.7 0.0 copy-done.1
  74.7 0.0 all-reduce.9.cloned.1.call-update
  74.8 0.6 copy-done.18
  75.4 0.7 constant_dynamic-slice_fusion.1
  81.1 0.0 copy-done.17
  81.2 0.7 fusion.49
  86.8 0.3 broadcast_in_dim.7
  87.0 2.2 bitcast_multiply_fusion.1
  89.2 112.1 %all-reduce.9.cloned.1.call-done = (f32[1,512,1024]{1,2,0:T(8,128)}, f32[1,512,1024]{1,2,0:T(8,128)}, f32[1,512,1024]{1,2,0:T(8,128)}, f32[1,512,1024]{1,2,0:T(8,128)}) async-done(((f32[1,512,1024]{1,2,0:T(8,128)}, f32[1,512,1024]{1,2,0:T(8,128)}, f32[1,512,1024]{1,2,0:T(8,128)}, f32[1,512,1024]{1,2,0:T(8,128)}), (f32[1,512,1024]{1,2,0:T(8,128)}, f32[1,512,1024]{1,2,0:T(8,128)}, f32[1,512,1024]{1,2,0:T(8,128)}, ...) | async-done | bytes 8388624 | tf_op jit(solution)/shard_map/psum | solution.py:15
  201.4 1.9 constant_dynamic-update-slice_fusion.3
  203.3 0.3 copy-done.10
  203.6 0.2 constant_dynamic-update-slice_fusion.2
  203.8 1.4 copy-done.9
  205.2 0.2 constant_dynamic-update-slice_fusion.1
  205.3 1.4 copy-done.8
  206.8 0.2 constant_dynamic-update-slice_fusion
  206.9 3.5 fusion.2
  210.5 4.6 fusion.6
  215.0 4.9 fusion.10
  219.9 0.0 copy-done.2
  219.9 4.5 fusion.14
  224.4 2.7 copy.24
  227.1 1.3 copy.25
  228.5 1.3 copy.26
  229.8 1.3 copy.27
  231.1 9.2 %fusion.8 = f32[512,1024]{1,0:T(8,128)S(1)} fusion(f32[4,512,1024]{1,2,0:T(8,128)} %copy-done.2, s32[]{:T(128)} %bitcast.18, f32[512,512]{1,0:T(8,128)S(1)} %copy-done.5, f32[512]{0:T(512)S(1)} %get-tuple-element.11, f32[512]{0:T(512)S(1)} %copy-done.19, f32[512,512]{0,1:T(8,128)} %copy.25), kind=kOutput, calls=%fused_computation.9 | convolution fusion | flops 3222798336 | bytes 6300160 | tf_op jit(solution)/shard_map/dot_general | solution.py:34
  240.3 0.0 copy-done.13
  240.3 0.0 slice-start.1
  240.3 0.0 copy-start.11
  240.3 8.7 %fusion.4 = f32[512,1024]{1,0:T(8,128)S(1)} fusion(f32[4,512,1024]{1,2,0:T(8,128)} %copy-done.2, s32[]{:T(128)} %bitcast.23, f32[512,512]{1,0:T(8,128)S(1)} %copy-done.3, f32[512]{0:T(512)S(1)} %get-tuple-element.13, f32[512]{0:T(512)S(1)} %copy-done.19, f32[512,512]{0,1:T(8,128)S(1)} %copy-done.13), kind=kOutput, calls=%fused_computation.5 | convolution fusion | flops 3222798336 | bytes 6300160 | tf_op jit(solution)/shard_map/dot_general | solution.py:34
  249.0 0.0 slice-done
  249.0 0.0 slice-done.1
  249.1 0.0 copy-done.11
  249.1 0.0 copy-start.7
  249.1 7.2 %fusion = f32[512,1024]{1,0:T(8,128)S(1)} fusion(f32[4,512,1024]{1,2,0:T(8,128)S(1)} %bitcast.112, s32[]{:T(128)} %bitcast.28, f32[512,512]{1,0:T(8,128)S(1)} %fusion.2, f32[512]{0:T(512)S(1)} %get-tuple-element.12, f32[512]{0:T(512)S(1)} %copy-done.19, f32[512,512]{0,1:T(8,128)S(1)} %copy-done.11), kind=kOutput, calls=%fused_computation.1 | convolution fusion | flops 3222798336 | bytes 6299652 | tf_op jit(solution)/shard_map/dot_general | solution.py:34
  256.3 7.2 %add_bitcast_fusion = f32[1,512,1024]{2,1,0:T(8,128)S(1)} fusion(f32[512,1024]{1,0:T(8,128)S(1)} %fusion, f32[512,1024]{1,0:T(8,128)S(1)} %fusion.4, f32[512,1024]{1,0:T(8,128)S(1)} %fusion.8, f32[4,512,1024]{1,2,0:T(8,128)S(1)} %bitcast.112, s32[]{:T(128)} %bitcast.13, f32[]{:T(128)} %bitcast.27, f32[]{:T(128)} %bitcast.22, f32[]{:T(128)} %bitcast.17, ...), kind=kOutput, calls=%fused_computation.18 | convolution fusion | flops 3226468352 | bytes 12591124 | tf_op jit(solution)/shard_map/dot_general | solution.py:34
  263.5 3.7 copy.28
  267.2 6.7 %all-to-all-start.1 = ((f32[1,512,1024]{1,0,2:T(1,128)}), f32[1,512,1024]{1,0,2:T(1,128)S(1)}, u32[]{:S(2)}, u32[]{:S(2)}) async-start(f32[1,512,1024]{1,0,2:T(1,128)} %copy.28), calls=%async_computation.1 | async-start | bytes 4194304 | tf_op jit(solution)/shard_map/all_to_all | solution.py:78
  273.9 0.3 all-reduce.5.cloned.1.call-start
  274.2 4.5 convolution_multiply_fusion.3
  278.7 2.5 fusion.28
  281.2 0.0 copy-start.12
  281.3 2.5 fusion.27
  283.8 3.5 fusion.26
  287.2 0.0 all-reduce.5.cloned.1.call-update
  287.3 0.0 all-reduce.7.cloned.1.call-start
  287.3 82.9 %all-reduce.5.cloned.1.call-done = f32[512,512]{1,0:T(8,128)} async-done(((f32[512,512]{1,0:T(8,128)}), f32[512,512]{1,0:T(8,128)}) %all-reduce.5.cloned.1.call-update) | async-done | bytes 1048592 | tf_op jit(solution)/shard_map/psum | solution.py:79
  370.3 0.0 all-reduce.7.cloned.1.call-update
  370.3 121.4 %all-reduce.7.cloned.1.call-done = f32[512,512]{1,0:T(8,128)} async-done(((f32[512,512]{1,0:T(8,128)}), f32[512,512]{1,0:T(8,128)}) %all-reduce.7.cloned.1.call-update) | async-done | bytes 1048592 | tf_op jit(solution)/shard_map/psum | solution.py:79
  491.7 2.3 broadcast_multiply_fusion
  494.0 0.0 all-to-all-done.1
  494.0 3.6 copy.29
  (30 shorter events, 0.1 us)
Async XLA Ops:
  7.2 12.0 %copy-start = (s32[256,8,16]{0,2,1:T(8,128)S(1)}, s32[256,8,16]{0,2,1:T(8,128)}, u32[]{:S(2)}) copy-start(s32[256,8,16]{0,2,1:T(8,128)} %param.8) | copy-start | bytes 393220
  10.1 60.7 %all-to-all-start = ((f32[8,512,128]{1,2,0:T(8,128)}), f32[8,512,128]{1,2,0:T(8,128)S(1)}, u32[]{:S(2)}, u32[]{:S(2)}) async-start(f32[8,512,128]{1,2,0:T(8,128)} %copy.21), calls=%async_computation | async-start | bytes 4194304 | tf_op jit(solution)/shard_map/all_to_all | solution.py:53
  19.1 182.3 %all-reduce.9.cloned.1.call-start = ((), (), s32[]{:S(2)}) async-start(), calls=%async_computation.4 | async-start | bytes 16777216 | tf_op jit(solution)/shard_map/psum | solution.py:15
  70.8 4.0 copy-start.1
  74.7 0.7 copy-start.18
  74.7 6.4 %copy-start.17 = (f32[256]{0:T(256)S(1)}, f32[256]{0:T(256)}, u32[]{:S(2)}) copy-start(f32[256]{0:T(256)} %param.6) | copy-start | bytes 3076
  74.7 12.0 %copy-start.19 = (f32[512]{0:T(512)S(1)}, f32[512]{0:T(512)}, u32[]{:S(2)}) copy-start(f32[512]{0:T(512)} %param.7) | copy-start | bytes 6148
  201.4 2.2 copy-start.10
  203.6 1.6 copy-start.9
  205.2 1.6 copy-start.8
  206.9 13.0 %copy-start.2 = (f32[4,512,1024]{1,2,0:T(8,128)}, f32[4,512,1024]{1,2,0:T(8,128)S(1)}, u32[]{:S(2)}) copy-start(f32[4,512,1024]{1,2,0:T(8,128)S(1)} %constant_dynamic-update-slice_fusion) | copy-start | bytes 25165828
  224.4 2.7 copy-start.5
  224.4 4.0 copy-start.3
  231.1 9.2 %copy-start.13 = (f32[512,512]{0,1:T(8,128)S(1)}, f32[512,512]{0,1:T(8,128)}, u32[]{:S(2)}) copy-start(f32[512,512]{0,1:T(8,128)} %copy.26) | copy-start | bytes 3145732
  231.1 17.9 %slice-start = ((s8[8388608]{0:T(1024)(128)(4,1)}), s8[4194304]{0:T(1024)(128)(4,1)S(1)}, s32[]{:S(2)}) async-start(s8[8388608]{0:T(1024)(128)(4,1)} %bitcast.111), calls=%async_computation.5 | async-start | bytes 8388608
  240.3 8.7 %slice-start.1 = ((s8[8388608]{0:T(1024)(128)(4,1)}), s8[4194304]{0:T(1024)(128)(4,1)S(1)}, s32[]{:S(2)}) async-start(s8[8388608]{0:T(1024)(128)(4,1)} %bitcast.111), calls=%async_computation.6 | async-start | bytes 8388608
  240.3 8.7 %copy-start.11 = (f32[512,512]{0,1:T(8,128)S(1)}, f32[512,512]{0,1:T(8,128)}, u32[]{:S(2)}) copy-start(f32[512,512]{0,1:T(8,128)} %copy.27) | copy-start | bytes 3145732
  249.1 7.2 %copy-start.7 = (f32[512,512]{1,0:T(8,128)S(1)}, f32[512,512]{1,0:T(8,128)}, u32[]{:S(2)}) copy-start(f32[512,512]{1,0:T(8,128)} %fusion.14) | copy-start | bytes 3145732
  249.1 7.2 %copy-start.16 = (f32[512,512]{0,1:T(8,128)S(1)}, f32[512,512]{0,1:T(8,128)}, u32[]{:S(2)}) copy-start(f32[512,512]{0,1:T(8,128)} %copy.24) | copy-start | bytes 3145732
  267.2 226.8 %all-to-all-start.1 = ((f32[1,512,1024]{1,0,2:T(1,128)}), f32[1,512,1024]{1,0,2:T(1,128)S(1)}, u32[]{:S(2)}, u32[]{:S(2)}) async-start(f32[1,512,1024]{1,0,2:T(1,128)} %copy.28), calls=%async_computation.1 | async-start | bytes 4194304 | tf_op jit(solution)/shard_map/all_to_all | solution.py:78
  273.9 96.4 %all-reduce.5.cloned.1.call-start = ((), (), s32[]{:S(2)}) async-start(), calls=%async_computation.2 | async-start | bytes 2097152 | tf_op jit(solution)/shard_map/psum | solution.py:79
  274.2 4.5 copy-start.6
  274.2 4.5 copy-start.15
  278.7 2.5 copy-start.4
  278.7 2.5 copy-start.14
  281.2 2.5 copy-start.12
  287.3 204.4 %all-reduce.7.cloned.1.call-start = ((), (), s32[]{:S(2)}) async-start(), calls=%async_computation.3 | async-start | bytes 2097152 | tf_op jit(solution)/shard_map/psum | solution.py:79
Sparse Core Ops, SparseCore 0:
  74.9 126.4 all-reduce.8
  287.4 82.8 all-reduce.4
  373.5 118.1 all-reduce.6
